TPU v7x, 32 devices: a whole 2x2x4 slice. The times are simulated.
32 devices in a mesh: groups: 2 (over y), expert: 4 (over z), replica: 4 (over x, core).
Axes of the slice: x: 2, y: 2, z: 4, core: 2. Of those that a mesh axis runs over, the one named last changes fastest.
Arguments:
- tokens: bfloat16 [4096, 1024], P(('groups', 'expert', 'replica')), parts along dimension 0, may hold values from -6 to 6
- expert_ids: int32 [4096, 6], P(('groups', 'expert', 'replica')), parts along dimension 0, may hold values from 0 to 15, all different within a row; in each aligned block of 128 rows (0 to 127, 128 to 255, ...) at most 64 rows name the same one
- gate_probs: bfloat16 [4096, 6], P(('groups', 'expert', 'replica')), parts along dimension 0, may hold values from 0.099609375 to 0.59765625
- cotangent: bfloat16 [4096, 1024], P(('groups', 'expert', 'replica')), parts along dimension 0, may hold values from -1.5 to 1.5
- gate_up: bfloat16 [1024, 16, 1536], P(None, 'expert'), may hold values from -0.1875 to 0.1875
- down_weights: bfloat16 [768, 16, 1024], P(None, 'expert'), may hold values from -0.21875 to 0.21875
Outputs:
- combined: bfloat16 [4096, 1024], P(('groups', 'expert', 'replica')), parts along dimension 0
- token_gradient: bfloat16 [4096, 1024], P(('groups', 'expert', 'replica')), parts along dimension 0
- prob_gradient: float32 [4096, 6], P(('groups', 'expert', 'replica')), parts along dimension 0
- gate_up_gradient: float32 [2048, 16, 1536], P(('groups', 'replica'), 'expert'), parts along dimension 0
- down_gradient: float32 [1536, 16, 1024], P(('groups', 'replica'), 'expert'), parts along dimension 0
There are 2 independent parts, one for each index of `groups`. A program takes and returns all parts, laid end to end along the dimension named above; an argument that names none is the same for every part. Nothing has to cross between parts.
Inputs may be any that keep to these rules, and one draw needn't show every extreme that they name: `expert_ids`: each row names 6 different experts. Within the rows of one device (aligned blocks of 128 rows) no expert is named by more than 64 rows, and in some block one expert is named by exactly 64 rows.
All inputs are finite; a program needn't handle non-finite values.
Results may differ from a plain program's by a relative error of at most 0.0064.
Values may be sent and summed in bfloat16 or wider, within the bound.
A program may use at most 128 MiB of HBM per device.

v0:
```python
import jax
import jax.numpy as jnp
from jax import lax
from jax.sharding import PartitionSpec as P

EXPERTS = 16
CAP = 64


def slot_table(expert_ids, experts, capacity):
    flat_ids = expert_ids.reshape(-1)
    assigned = flat_ids.shape[0]
    onehot = (flat_ids[:, None] == jnp.arange(experts, dtype=jnp.int32)[None, :]).astype(jnp.int32)
    before = jnp.cumsum(onehot, axis=0) - onehot
    slot_index = jnp.sum(before * onehot, axis=1)
    position = (flat_ids * capacity + slot_index).astype(jnp.int32)
    slot_owner = (
        jnp.full((experts * capacity,), assigned, jnp.int32)
        .at[position]
        .set(jnp.arange(assigned, dtype=jnp.int32))
    )
    return (position, slot_owner)


def expert_forward(received, gate_up, down_weights):
    local_count = gate_up.shape[1]
    blocks = received.reshape(
        received.shape[0] // local_count, local_count, received.shape[1], received.shape[2]
    )
    pre_act = jnp.einsum("secd,def->secf", blocks, gate_up, preferred_element_type=jnp.float32)
    middle = pre_act.shape[-1] // 2
    hidden = (jax.nn.silu(pre_act[..., :middle]) * pre_act[..., middle:]).astype(jnp.bfloat16)
    outputs = jnp.einsum(
        "secf,fed->secd", hidden, down_weights, preferred_element_type=jnp.float32
    ).astype(jnp.bfloat16)
    return (outputs.reshape(received.shape), pre_act, hidden)


def on_device(tokens, expert_ids, gate_probs, cotangent, gate_up, down_weights):
    tok_count, model_width = tokens.shape
    per_patch = expert_ids.shape[1]
    local_count = gate_up.shape[1]
    sources = EXPERTS // local_count
    position, slot_owner = slot_table(expert_ids, EXPERTS, CAP)
    all_tokens, all_ids = (
        lax.all_gather(tokens, "expert", axis=0, tiled=True),
        lax.all_gather(expert_ids, "expert", axis=0, tiled=True),
    )
    first_expert = lax.axis_index("expert") * local_count
    owner_tables = jax.vmap(lambda choose: slot_table(choose, EXPERTS, CAP)[1])(
        all_ids.reshape(sources, tok_count, per_patch)
    )
    mine = lax.dynamic_slice_in_dim(
        owner_tables.reshape(sources, EXPERTS, CAP), first_expert, local_count, 1
    ).reshape(sources, local_count * CAP)
    source_zeros = jnp.zeros((sources, 1, model_width), jnp.bfloat16)
    source_tokens = jnp.concatenate(
        [all_tokens.reshape(sources, tok_count, model_width), source_zeros], axis=1
    )
    received = jax.vmap(lambda values, owners: values[owners // per_patch])(
        source_tokens, mine
    ).reshape(EXPERTS, CAP, model_width)
    outputs, pre_act, hidden = expert_forward(received, gate_up, down_weights)
    returned = lax.all_to_all(outputs, "expert", split_axis=0, concat_axis=0, tiled=True)
    picked = (
        returned.reshape(EXPERTS * CAP, model_width)[position]
        .reshape(tok_count, per_patch, model_width)
        .astype(jnp.float32)
    )
    probs_float = gate_probs.astype(jnp.float32)
    combined = jnp.sum(probs_float[:, :, None] * picked, axis=1).astype(jnp.bfloat16)
    cot_float = cotangent.astype(jnp.float32)
    prob_gradient = jnp.sum(cot_float[:, None, :] * picked, axis=2)
    all_cot, all_probs = (
        lax.all_gather(cotangent, "expert", axis=0, tiled=True),
        lax.all_gather(gate_probs, "expert", axis=0, tiled=True),
    )
    source_cot = jnp.concatenate(
        [all_cot.reshape(sources, tok_count, model_width), source_zeros], axis=1
    )
    zero_probs = jnp.zeros((sources, 1), jnp.bfloat16)
    source_probs = jnp.concatenate(
        [all_probs.reshape(sources, tok_count * per_patch), zero_probs], axis=1
    )
    cot_rows = jax.vmap(lambda values, owners: values[owners // per_patch])(source_cot, mine)
    prob_rows = jax.vmap(lambda values, owners: values[owners])(source_probs, mine)
    cot_received = (
        (prob_rows[:, :, None].astype(jnp.float32) * cot_rows.astype(jnp.float32))
        .astype(jnp.bfloat16)
        .reshape(EXPERTS, CAP, model_width)
    )
    block_shape = (sources, local_count, CAP, model_width)
    slot_inputs = received.reshape(block_shape)
    slot_cotangent = cot_received.reshape(block_shape)
    middle = pre_act.shape[-1] // 2
    gate_part = pre_act[..., :middle]
    up_part = pre_act[..., middle:]
    hidden_grad = jnp.einsum(
        "secd,fed->secf", slot_cotangent, down_weights, preferred_element_type=jnp.float32
    )
    sigmoid_gate = jax.nn.sigmoid(gate_part)
    pre_gradient = jnp.concatenate(
        [
            hidden_grad * up_part * sigmoid_gate * (1.0 + gate_part * (1.0 - sigmoid_gate)),
            hidden_grad * gate_part * sigmoid_gate,
        ],
        axis=-1,
    ).astype(jnp.bfloat16)
    input_grads = jnp.einsum(
        "secf,def->secd", pre_gradient, gate_up, preferred_element_type=jnp.float32
    ).astype(jnp.bfloat16)
    returned_grads = lax.all_to_all(
        input_grads.reshape(EXPERTS, CAP, model_width),
        "expert",
        split_axis=0,
        concat_axis=0,
        tiled=True,
    )
    token_rows = returned_grads.reshape(EXPERTS * CAP, model_width)[position].reshape(
        tok_count, per_patch, model_width
    )
    token_gradient = jnp.sum(token_rows.astype(jnp.float32), axis=1).astype(jnp.bfloat16)
    full_inner = jnp.einsum(
        "secd,secf->def", slot_inputs, pre_gradient, preferred_element_type=jnp.float32
    )
    full_down = jnp.einsum(
        "secf,secd->fed", hidden, slot_cotangent, preferred_element_type=jnp.float32
    )
    gate_up_gradient, down_gradient = (
        lax.psum_scatter(full_inner, "replica", scatter_dimension=0, tiled=True),
        lax.psum_scatter(full_down, "replica", scatter_dimension=0, tiled=True),
    )
    return (combined, token_gradient, prob_gradient, gate_up_gradient, down_gradient)


def solution(mesh):
    placed = (
        P(("groups", "expert", "replica"), None),
        P(("groups", "expert", "replica"), None),
        P(("groups", "expert", "replica"), None),
        P(("groups", "expert", "replica"), None),
        P(None, "expert", None),
        P(None, "expert", None),
    )
    return jax.shard_map(
        on_device,
        mesh=mesh,
        in_specs=placed,
        out_specs=(
            P(("groups", "expert", "replica"), None),
            P(("groups", "expert", "replica"), None),
            P(("groups", "expert", "replica"), None),
            P(("groups", "replica"), "expert", None),
            P(("groups", "replica"), "expert", None),
        ),
        check_vma=False,
    )
```

profile of v0, /device:TPU:0, one launch (start us, length us, event | category | flops | bytes accessed | tf_op | source)
XLA Modules:
  0.0 553.4 jit_solution(15946966605619337818)
XLA Ops:
  8.7 15.2 %all_gather.13 = s32[512,6]{0,1:T(8,128)S(1)} all-gather(s32[128,6]{0,1:T(8,128)} %param.7), channel_id=1, replica_groups=mesh['groups'=2,'expert'=4,'replica'=4] {'expert'}, dimensions={0}, use_global_device_ids=true | all-gather | bytes 15360 | tf_op jit(solution)/shard_map/all_gather | solution.py:47
  24.4 12.5 %all_gather.14 = bf16[512,6]{0,1:T(8,128)(2,1)S(1)} all-gather(bf16[128,6]{0,1:T(8,128)(2,1)} %param.8), channel_id=1, replica_groups=mesh['groups'=2,'expert'=4,'replica'=4] {'expert'}, dimensions={0}, use_global_device_ids=true | all-gather | bytes 7680 | tf_op jit(solution)/shard_map/all_gather | solution.py:76
  37.3 6.8 %reduce-window.14 = s32[4,16,6,128]{3,1,2,0:T(8,128)S(1)} reduce-window(s32[4,16,6,128]{3,1,2,0:T(8,128)S(1)} %fusion.28, s32[]{:T(128)} %constant.19.clone.1), window={size=1x1x1x128 pad=0_0x0_0x0_0x127_0}, to_apply=%region_0.0 | reduce-window | flops 6242304 | bytes 393220 | tf_op jit(solution)/shard_map/reduce-window
  45.2 11.8 %scatter_custom_fusion = s32[4096]{0:T(1024)S(1)} fusion(s32[3072]{0:T(1024)S(1)} %reshape.287, s32[3072]{0:T(1024)S(1)} %reshape.289, s32[]{:T(128)} %constant.17.clone.1), kind=kCustom, calls=%fused_computation.62 | custom fusion | bytes 16388
  57.2 9.2 %gather_fusion.3 = bf16[1024]{0:T(1024)(128)(2,1)S(1)} fusion(bf16[4,769]{1,0:T(4,128)(2,1)S(1)} %concatenate.14, s32[1024]{0:T(1024)S(1)} %bitcast.103), kind=kCustom, calls=%fused_computation.3 | custom fusion | bytes 12288 | tf_op jit(solution)/shard_map/vmap()/gather | solution.py:86
  72.3 15.2 %gather_fusion.4 = bf16[1024,1024]{1,0:T(8,128)(2,1)} fusion(bf16[4,129,1024]{2,0,1:T(4,128)(2,1)S(1)} %concatenate.15, s32[1024]{0:T(1024)S(1)} %bitcast.100), kind=kCustom, calls=%fused_computation.4 | custom fusion | bytes 4202496 | tf_op jit(solution)/shard_map/vmap()/gather | solution.py:85
  87.5 9.9 %gather_fusion.2 = bf16[1024,1024]{1,0:T(8,128)(2,1)S(1)} fusion(bf16[4,129,1024]{2,0,1:T(4,128)(2,1)S(1)} %concatenate.13, s32[1024]{0:T(1024)S(1)} %bitcast.101), kind=kCustom, calls=%fused_computation.2 | custom fusion | bytes 4202496 | tf_op jit(solution)/shard_map/vmap()/gather | solution.py:60
  97.4 9.2 %fusion.8 = f32[4,4,64,1536]{3,2,0,1:T(8,128)S(1)} fusion(bf16[1024,4,1536,1]{2,1,0,3:T(4,128)(2,1)} %bitcast.113, bf16[4,4,64,1024]{3,2,1,0:T(8,128)(2,1)S(1)} %bitcast.106), kind=kOutput, calls=%fused_computation.15 | convolution fusion | flops 3221225472 | bytes 20971520 | tf_op jit(solution)/shard_map/secd,def->secf/dot_general | solution.py:30
  106.7 10.2 %fusion.14 = (bf16[4,4,64,768]{3,2,0,1:T(8,128)(2,1)}, bf16[4,4,64,768]{3,2,0,1:T(8,128)(2,1)}, bf16[4,4,64,768]{3,2,0,1:T(8,128)(2,1)S(1)}) fusion(f32[4,4,64,1536]{3,2,0,1:T(8,128)S(1)} %fusion.8, bf16[768,4,1024,1]{2,1,0,3:T(4,128)(2,1)} %bitcast.115, f32[4,4,64]{2,0,1:T(4,128)S(1)} %copy.64, bf16[4,4,64,1024]{3,2,1,0:T(8,128)(2,1)S(1)} %bitcast.108), kind=kOutput, calls=%fused_computation.26 | convolution fusion | flops 1626341376 | bytes 19402752 | tf_op jit(solution)/shard_map/secd,fed->secf/dot_general | solution.py:98
  118.0 6.5 %convolution_bitcast_fusion.1 = f32[768,4,1024]{0,2,1:T(8,128)} fusion(bf16[4,4,64,768]{3,2,0,1:T(8,128)(2,1)S(1)} %get-tuple-element.24, f32[4,4,64]{2,0,1:T(4,128)S(1)} %copy.64, bf16[4,4,64,1024]{3,2,1,0:T(8,128)(2,1)S(1)} %bitcast.109), kind=kOutput, calls=%fused_computation.16 | convolution fusion | flops 1613758464 | bytes 16257024 | tf_op jit(solution)/shard_map/secf,secd->fed/dot_general | solution.py:126
  124.5 15.4 %copy.71 = f32[768,4,1024]{2,1,0:T(4,128)} copy(f32[768,4,1024]{0,2,1:T(8,128)} %convolution_bitcast_fusion.1) | data formatting | bytes 25165824 | tf_op jit(solution)/shard_map/secf,secd->fed/transpose | solution.py:126
  140.0 13.1 %convolution_bitcast_fusion = f32[1024,4,1536]{0,2,1:T(8,128)} fusion(bf16[4,4,64,768]{3,2,0,1:T(8,128)(2,1)} %get-tuple-element.23, bf16[4,4,64,768]{3,2,0,1:T(8,128)(2,1)} %get-tuple-element.22, bf16[4,4,64,1024]{3,2,1,0:T(8,128)(2,1)S(1)} %bitcast.107), kind=kOutput, calls=%fused_computation.6 | convolution fusion | flops 3227516928 | bytes 30408704 | tf_op jit(solution)/shard_map/secd,secf->def/dot_general | solution.py:123
  153.1 9.7 %convert_bitcast_fusion = bf16[4,4,64,1024]{3,2,0,1:T(8,128)(2,1)S(1)} fusion(bf16[1024,4,1536,1]{2,1,0,3:T(4,128)(2,1)} %bitcast.114, bf16[4,4,64,768]{3,2,0,1:T(8,128)(2,1)} %get-tuple-element.23, bf16[4,4,64,768]{3,2,0,1:T(8,128)(2,1)} %get-tuple-element.22), kind=kOutput, calls=%fused_computation.31 | convolution fusion | flops 3228565504 | bytes 17825792 | tf_op jit(solution)/shard_map/secf,def->secd/dot_general | solution.py:109
  164.5 3.6 all-to-all-start.1
  168.1 7.4 %convert_bitcast_fusion.1 = bf16[4,4,64,1024]{3,2,0,1:T(8,128)(2,1)S(1)} fusion(bf16[4,4,64,768]{3,2,0,1:T(8,128)(2,1)} %copy-done.7, bf16[768,4,1024,1]{2,1,0,3:T(4,128)(2,1)} %bitcast.116), kind=kOutput, calls=%fused_computation.32 | convolution fusion | flops 1611661312 | bytes 9961472 | tf_op jit(solution)/shard_map/secf,fed->secd/dot_general | solution.py:33
  177.0 39.2 %all-to-all-done.1 = bf16[16,64,1024]{2,1,0:T(8,128)(2,1)S(1)} async-done(((bf16[16,64,1024]{2,1,0:T(8,128)(2,1)}), bf16[16,64,1024]{2,1,0:T(8,128)(2,1)S(1)}, u32[]{:S(2)}, u32[]{:S(2)}) %all-to-all-start.1) | async-done | bytes 2097184 | tf_op jit(solution)/shard_map/all_to_all | solution.py:112
  216.1 4.7 all-to-all-start
  233.4 35.3 %all-to-all-done = bf16[16,64,1024]{2,1,0:T(8,128)(2,1)} async-done(((bf16[16,64,1024]{2,1,0:T(8,128)(2,1)}), bf16[16,64,1024]{2,1,0:T(8,128)(2,1)}, u32[]{:S(2)}, u32[]{:S(2)}) %all-to-all-start) | async-done | bytes 2097184 | tf_op jit(solution)/shard_map/all_to_all | solution.py:64
  268.7 5.7 %gather_fusion = bf16[768,1024]{1,0:T(8,128)(2,1)S(1)} fusion(bf16[1024,1024]{1,0:T(8,128)(2,1)} %bitcast.10, s32[1024]{0:T(1024)S(1)} %pad_clamp_fusion), kind=kCustom, calls=%fused_computation | custom fusion | bytes 3148800 | tf_op jit(solution)/shard_map/gather | solution.py:66
  276.6 4.8 multiply_reduce_fusion
  282.1 78.0 %all-reduce.6.cloned.1.call-done = f32[768,4,1024]{2,1,0:T(4,128)} async-done(((f32[768,4,1024]{2,1,0:T(4,128)}), f32[768,4,1024]{2,1,0:T(4,128)}) %all-reduce.6.cloned.1.call-update) | async-done | bytes 12582928
  360.2 4.2 constant_dynamic-slice_fusion
  364.4 174.1 %reduce-scatter.2.cloned.1.call-done = f32[256,4,1536]{0,2,1:T(8,128)} async-done(((f32[1024,4,1536]{0,2,1:T(8,128)}), f32[256,4,1536]{0,2,1:T(8,128)}) %reduce-scatter.2.cloned.1.call-update) | async-done | bytes 6291472 | tf_op jit(solution)/shard_map/reduce_scatter | solution.py:130
  538.5 7.9 %copy.73 = f32[256,4,1536]{2,1,0:T(4,128)} copy(f32[256,4,1536]{0,2,1:T(8,128)} %reduce-scatter.2.cloned.1.call-done) | data formatting | bytes 12582912
  (85 shorter events, 28.5 us)
Async XLA Ops:
  7.2 37.8 %copy-start.5 = (s32[2]{0:T(128)S(1)}, s32[2]{0:T(128)}, u32[]{:S(2)}) copy-start(s32[2]{0:T(128)} %constant.62) | copy-start | bytes 28
  7.2 37.9 %copy-start.4 = (s32[2]{0:T(128)S(1)}, s32[2]{0:T(128)}, u32[]{:S(2)}) copy-start(s32[2]{0:T(128)} %constant.65) | copy-start | bytes 28
  7.2 59.3 %all-gather.3.cloned.1.call-start = ((), (), s32[]{:S(2)}) async-start(), calls=%async_computation.3 | async-start | bytes 1310720 | tf_op jit(solution)/shard_map/all_gather | solution.py:46
  7.9 61.5 %all-gather.5.cloned.1.call-start = ((), (), s32[]{:S(2)}) async-start(), calls=%async_computation.4 | async-start | bytes 1310720 | tf_op jit(solution)/shard_map/all_gather | solution.py:75
  8.7 351.5 %all-reduce.6.cloned.1.call-start = ((), (), s32[]{:S(2)}) async-start(), calls=%async_computation.6 | async-start | bytes 25165824
  97.4 9.3 %copy-start = (bf16[1024,1024]{1,0:T(8,128)(2,1)S(1)}, bf16[1024,1024]{1,0:T(8,128)(2,1)}, u32[]{:S(2)}) copy-start(bf16[1024,1024]{1,0:T(8,128)(2,1)} %gather_fusion.4) | copy-start | bytes 6291460
  116.9 1.1 copy-start.7
  140.0 398.5 %reduce-scatter.2.cloned.1.call-start = ((), (), s32[]{:S(2)}) async-start(), calls=%async_computation.5 | async-start | bytes 31457280 | tf_op jit(solution)/shard_map/reduce_scatter | solution.py:130
  164.5 51.7 %all-to-all-start.1 = ((bf16[16,64,1024]{2,1,0:T(8,128)(2,1)}), bf16[16,64,1024]{2,1,0:T(8,128)(2,1)S(1)}, u32[]{:S(2)}, u32[]{:S(2)}) async-start(bf16[16,64,1024]{2,1,0:T(8,128)(2,1)} %bitcast.105), calls=%async_computation.1 | async-start | bytes 4194304 | tf_op jit(solution)/shard_map/all_to_all | solution.py:112
  177.0 43.9 %copy-start.2 = (s32[128,6]{0,1:T(8,128)S(1)}, s32[128,6]{0,1:T(8,128)}, u32[]{:S(2)}) copy-start(s32[128,6]{0,1:T(8,128)} %param.7) | copy-start | bytes 9220
  177.0 44.3 %copy-start.3 = (bf16[128,6]{0,1:T(8,128)(2,1)S(1)}, bf16[128,6]{0,1:T(8,128)(2,1)}, u32[]{:S(2)}) copy-start(bf16[128,6]{0,1:T(8,128)(2,1)} %param.8) | copy-start | bytes 4612
  177.0 44.5 %copy-start.1 = (bf16[128,1024]{1,0:T(8,128)(2,1)S(1)}, bf16[128,1024]{1,0:T(8,128)(2,1)}, u32[]{:S(2)}) copy-start(bf16[128,1024]{1,0:T(8,128)(2,1)} %param.9) | copy-start | bytes 786436
  177.0 46.8 %copy-start.6 = (u32[32]{0:T(128)S(1)}, u32[32]{0:T(128)}, u32[]{:S(2)}) copy-start(u32[32]{0:T(128)} %constant.111) | copy-start | bytes 388
  216.1 52.6 %all-to-all-start = ((bf16[16,64,1024]{2,1,0:T(8,128)(2,1)}), bf16[16,64,1024]{2,1,0:T(8,128)(2,1)}, u32[]{:S(2)}, u32[]{:S(2)}) async-start(bf16[16,64,1024]{2,1,0:T(8,128)(2,1)} %bitcast.104), calls=%async_computation | async-start | bytes 4194304 | tf_op jit(solution)/shard_map/all_to_all | solution.py:64
Sparse Core Ops, SparseCore 0:
  9.6 30.9 all-gather.2
  42.1 27.3 all-gather.4
  140.1 220.0 all-reduce.5
  362.6 175.8 reduce-scatter.1
where the time goes:
time: 563 us; the launch traced here: 553 us
  waiting for transfers between devices  329 us (58%)
  local copies, waits for them, and re-layouts  101 us (18%)
  matrix products  56.2 us (10%)
  blocking collectives  27.6 us (5%)
  other arithmetic  16.1 us (3%)
  between operations  15.2 us (3%)
  starting transfers between devices  8.52 us (2%)
    reduce_scatter x1, waiting for transfers between devices, on_device(): lax.psum_scatter(full_inner, 'replica', scatter_dimension=0, tiled=True)  174 us
    unnamed x5, waiting for transfers between devices  79.4 us
    all_to_all x1, waiting for transfers between devices, on_device(): lax.all_to_all(input_grads.reshape(EXPERTS, CAP, model_width), 'expert',...  39.2 us
    all_to_all x1, waiting for transfers between devices, on_device(): lax.all_to_all(outputs, 'expert', split_axis=0, concat_axis=0, tiled=True)  35.3 us
    unnamed x26, local copies, waits for them, and re-layouts  26.5 us
    gather x2, local copies, waits for them, and re-layouts, on_device(): values[owners // per_patch]  25 us
    transpose x1, local copies, waits for them, and re-layouts, on_device(): jnp.einsum('secf,secd->fed', hidden, slot_cotangent, preferred_element_ty...  15.4 us
    all_gather x1, blocking collectives, on_device(): lax.all_gather(expert_ids, 'expert', axis=0, tiled=True)  15.2 us
  transfers between devices with their start and end apart: 6, of which 5 were waited for; matrix products, arithmetic and copies ran while one was open for 17% of the time, Pallas kernels for 0%

commit v1 on v0

v1 whole, which is shorter than its diff:
```python
import jax
import jax.numpy as jnp
from jax import lax
from jax.sharding import PartitionSpec as P

CAP = 64
CORES = 2
BF = jnp.bfloat16
F32 = jnp.float32


def on_device(tokens, expert_ids, gate_probs, cotangent, gate_up, down_weights, *, sources, replicas):
    count, width = tokens.shape
    top = expert_ids.shape[1]
    local = gate_up.shape[1]
    hidden_width = down_weights.shape[0]
    cap = min(CAP, count)
    along = replicas // CORES
    replica = lax.axis_index("replica")
    core, place = lax.rem(replica, CORES), lax.div(replica, CORES)
    first = lax.axis_index("expert") * local
    slots = sources * cap

    all_ids = lax.all_gather(expert_ids.T, "expert", axis=0)
    all_probs = lax.all_gather(gate_probs.T, "expert", axis=0)
    all_tokens = lax.all_gather(tokens, "expert", axis=0, tiled=True)
    all_cot = lax.all_gather(cotangent, "expert", axis=0, tiled=True)

    named = (all_ids[None] == (first + jnp.arange(local, dtype=jnp.int32))[:, None, None, None])
    member = jnp.any(named, axis=2)
    weight = jnp.sum(jnp.where(named, all_probs[None].astype(F32), 0.0), axis=2)
    ahead = (jnp.arange(count)[:, None] < jnp.arange(count)[None, :]).astype(BF)
    rank = jnp.einsum("esp,pq->esq", member.astype(BF), ahead, preferred_element_type=F32)
    rank = jnp.where(member, rank.astype(jnp.int32), -1)
    chosen = rank[:, :, None, :] == jnp.arange(cap, dtype=jnp.int32)[None, None, :, None]
    same = jnp.arange(sources)[:, None] == jnp.arange(sources)[None, :]
    wide = chosen[:, :, :, None, :] & same[None, :, None, :, None]
    pick = wide.astype(BF).reshape(local * slots, sources * count)
    back = jnp.where(wide, weight[:, :, None, None, :], 0.0).astype(BF).reshape(local * slots, sources * count)
    slot_weight = jnp.sum(jnp.where(chosen, weight[:, :, None, :], 0.0), axis=3).reshape(local, slots, 1)

    def rows(values):
        return jnp.dot(pick, values, preferred_element_type=F32).astype(BF).reshape(local, slots, width)

    inputs = rows(all_tokens)
    raw_cot = rows(all_cot)
    out_grad = (slot_weight * raw_cot.astype(F32)).astype(BF)

    pair = [(i, i ^ 1) for i in range(replicas)]

    def swap(values):
        return lax.ppermute(values, "replica", pair)

    def columns(values, shift, side):
        size = values.shape[-1] // replicas
        block = lax.rem(place + shift, along) * CORES + side
        return lax.dynamic_slice_in_dim(values, block * size, size, 2)

    def shared_columns(values):
        theirs = swap(jnp.concatenate([columns(values, s, 1 - core) for s in range(along)], axis=2))
        size = values.shape[-1] // replicas
        return [
            jnp.concatenate([columns(values, s, core), theirs[:, :, s * size:(s + 1) * size]], axis=1)
            for s in range(along)
        ]

    def shared(values):
        return jnp.concatenate([values, swap(values)], axis=1)

    def summed(left, right):
        total = None
        for shift in list(range(1, along)) + [0]:
            part = jnp.einsum("era,erb->eab", left[shift], right, preferred_element_type=F32)
            if shift:
                step = [
                    (x * CORES + c, ((x + shift) % along) * CORES + c)
                    for x in range(along) for c in range(CORES)
                ]
                part = lax.ppermute(part.astype(BF), "replica", step).astype(F32)
            total = part if total is None else total + part
        return total.swapaxes(0, 1)

    input_columns = shared_columns(inputs)
    both_grad = shared(out_grad)

    pre_act = jnp.einsum("erd,def->erf", inputs, gate_up, preferred_element_type=F32)
    gate, up = pre_act[..., :hidden_width], pre_act[..., hidden_width:]
    sig = jax.nn.sigmoid(gate)
    hidden = (gate * sig * up).astype(BF)
    down_gradient = summed(shared_columns(hidden), both_grad)

    hidden_grad = jnp.einsum("erd,fed->erf", out_grad, down_weights, preferred_element_type=F32)
    pre_grad = jnp.concatenate(
        [hidden_grad * up * sig * (1.0 + gate * (1.0 - sig)), hidden_grad * gate * sig], axis=-1
    ).astype(BF)
    gate_up_gradient = summed(input_columns, shared(pre_grad))

    outputs = jnp.einsum("erf,fed->erd", hidden, down_weights, preferred_element_type=F32).astype(BF)
    input_grad = jnp.einsum("erf,def->erd", pre_grad, gate_up, preferred_element_type=F32).astype(BF)

    def returned(matrix, values):
        part = jnp.einsum(
            "ra,rd->ad", matrix, values.reshape(local * slots, width), preferred_element_type=F32
        ).astype(BF).reshape(sources, count, width)
        arrived = lax.all_to_all(part, "expert", split_axis=0, concat_axis=0, tiled=True)
        return jnp.sum(arrived.astype(F32), axis=0).astype(BF)

    combined = returned(back, outputs)
    token_gradient = returned(pick, input_grad)

    slot_prob = jnp.sum(raw_cot.astype(F32) * outputs.astype(F32), axis=2).reshape(local, sources, cap, 1)
    prob_part = jnp.sum(jnp.where(chosen, slot_prob, 0.0), axis=2).swapaxes(0, 1)
    prob_all = lax.all_to_all(prob_part, "expert", split_axis=0, concat_axis=0, tiled=True)
    prob_all = prob_all.reshape(sources * local, count)
    mine = expert_ids.T[:, None, :] == jnp.arange(sources * local, dtype=jnp.int32)[None, :, None]
    prob_gradient = jnp.sum(jnp.where(mine, prob_all[None], 0.0), axis=1).T
    return (combined, token_gradient, prob_gradient, gate_up_gradient, down_gradient)


def solution(mesh):
    rows = P(("groups", "expert", "replica"), None)
    sources, replicas = mesh.shape["expert"], mesh.shape["replica"]

    def body(*args):
        return on_device(*args, sources=sources, replicas=replicas)

    return jax.shard_map(
        body,
        mesh=mesh,
        in_specs=(rows, rows, rows, rows, P(None, "expert", None), P(None, "expert", None)),
        out_specs=(
            rows,
            rows,
            rows,
            P(("groups", "replica"), "expert", None),
            P(("groups", "replica"), "expert", None),
        ),
        check_vma=False,
    )
```

time: 563 us -> 257 us (0.46)
  waiting for transfers between devices: 329 us -> 87.1 us
  local copies, waits for them, and re-layouts: 101 us -> 27.3 us
  matrix products: 56.2 us -> 68.9 us
  starting transfers between devices: 8.52 us -> 14.9 us
    reduce_scatter x1 -> x0, waiting for transfers between devices: 174 us -> none  [on_device(): lax.psum_scatter(full_inner, 'replica', scatter_dimension=0, tiled=True)]
    unnamed x5 -> x2, waiting for transfers between devices: 79.4 us -> 1.38 us
    all_to_all x2 -> x3, waiting for transfers between devices: 74.5 us -> 27.5 us  [the longest x2 27.5 us: returned(): lax.all_to_all(part, 'expert', split_axis=0, concat_axis=0, tiled=True)]
    gather x5 -> x0, local copies, waits for them, and re-layouts: 43.5 us -> none  [the longest x2 25 us: on_device(): values[owners // per_patch]]
    ppermute x0 -> x6, waiting for transfers between devices: none -> 42 us  [the longest x2 42 us: summed(): part = lax.ppermute(part.astype(BF), 'replica', step).astype(F32)]
    all_gather x2, waiting for transfers between devices: 0.93 us -> 16.2 us  [the longest x1 12.9 us: on_device(): all_cot = lax.all_gather(cotangent, 'expert', axis=0, tiled=True)]
    transpose x1, local copies, waits for them, and re-layouts: 15.4 us -> 0.6 us  [on_device(): jnp.sum(jnp.where(chosen, slot_prob, 0.0), axis=2).swapaxes(0, 1)]
    dot_general x6 -> x13, matrix products: 56.2 us -> 68.9 us  [the longest x4 17.3 us: summed(): jnp.einsum('era,erb->eab', left[shift], right, preferred_element_type=F32)]
  transfers between devices with their start and end apart: 6 -> 11, of which waited for: 5 -> 5; matrix products, arithmetic and copies ran while one was open for 17% -> 27% of each run, Pallas kernels for 0% -> 0%
where the time goes in v1:
time: 257 us; the launch traced here: 253 us
  waiting for transfers between devices  87.1 us (34%)
  matrix products  68.9 us (27%)
  blocking collectives  27.4 us (11%)
  local copies, waits for them, and re-layouts  27.3 us (11%)
  starting transfers between devices  14.9 us (6%)
  between operations  14.8 us (6%)
  other arithmetic  12.1 us (5%)
    ppermute x2, waiting for transfers between devices, summed(): part = lax.ppermute(part.astype(BF), 'replica', step).astype(F32)  42 us
    all_to_all x2, waiting for transfers between devices, returned(): lax.all_to_all(part, 'expert', split_axis=0, concat_axis=0, tiled=True)  27.5 us
    unnamed x38, local copies, waits for them, and re-layouts  17.5 us
    dot_general x4, matrix products, summed(): jnp.einsum('era,erb->eab', left[shift], right, preferred_element_type=F32)  17.3 us
    all_gather x1, blocking collectives, on_device(): all_probs = lax.all_gather(gate_probs.T, 'expert', axis=0)  13.8 us
    all_gather x1, blocking collectives, on_device(): all_ids = lax.all_gather(expert_ids.T, 'expert', axis=0)  13.7 us
    all_gather x1, waiting for transfers between devices, on_device(): all_cot = lax.all_gather(cotangent, 'expert', axis=0, tiled=True)  12.9 us
    dot_general x1, matrix products, on_device(): jnp.einsum('erd,fed->erf', out_grad, down_weights, preferred_element_type...  10.8 us
  transfers between devices with their start and end apart: 11, of which 5 were waited for; matrix products, arithmetic and copies ran while one was open for 27% of the time, Pallas kernels for 0%

profile of v1, /device:TPU:0, one launch (start us, length us, event | category | flops | bytes accessed | tf_op | source)
XLA Modules:
  0.0 252.5 jit_solution(17486382146186522078)
XLA Ops:
  8.7 13.8 %all-gather.3 = bf16[4,6,128]{2,1,0:T(8,128)(2,1)S(1)} all-gather(bf16[1,6,128]{2,1,0:T(8,128)(2,1)} %bitcast.66), channel_id=3, replica_groups=mesh['groups'=2,'expert'=4,'replica'=4] {'expert'}, dimensions={0}, use_global_device_ids=true | all-gather | bytes 7680 | tf_op jit(solution)/shard_map/all_gather | solution.py:25
  22.5 13.7 %all-gather.2 = s32[4,6,128]{2,1,0:T(8,128)S(1)} all-gather(s32[1,6,128]{2,1,0:T(8,128)} %bitcast.63), channel_id=2, replica_groups=mesh['groups'=2,'expert'=4,'replica'=4] {'expert'}, dimensions={0}, use_global_device_ids=true | all-gather | bytes 15360 | tf_op jit(solution)/shard_map/all_gather | solution.py:24
  37.3 3.3 %all-gather.7.cloned.1.call-done = bf16[512,1024]{1,0:T(8,128)(2,1)} async-done(((bf16[128,1024]{1,0:T(8,128)(2,1)}), bf16[512,1024]{1,0:T(8,128)(2,1)}) %all-gather.7.cloned.1.call-update) | async-done | bytes 1048592 | tf_op jit(solution)/shard_map/all_gather | solution.py:26
  40.5 2.5 fusion.19
  43.0 9.9 %fusion.2 = f32[4,256,1536]{2,1,0:T(8,128)S(1)} fusion(bf16[4,256,1024]{2,1,0:T(8,128)(2,1)S(1)} %bitcast.55, bf16[1024,4,1536]{2,1,0:T(4,128)(2,1)} %param.10), kind=kOutput, calls=%fused_computation.2 | convolution fusion | flops 3221225472 | bytes 20971520 | tf_op jit(solution)/shard_map/erd,def->erf/dot_general | solution.py:86
  52.9 2.7 %copy-done = f32[4,256,1536]{2,1,0:T(8,128)} copy-done((f32[4,256,1536]{2,1,0:T(8,128)}, f32[4,256,1536]{2,1,0:T(8,128)S(1)}, u32[]{:S(2)}) %copy-start) | copy-done | bytes 6291480
  56.6 12.9 %all-gather.9.cloned.1.call-done = bf16[512,1024]{1,0:T(8,128)(2,1)} async-done(((bf16[128,1024]{1,0:T(8,128)(2,1)}), bf16[512,1024]{1,0:T(8,128)(2,1)}) %all-gather.9.cloned.1.call-update) | async-done | bytes 1048592 | tf_op jit(solution)/shard_map/all_gather | solution.py:27
  72.0 9.1 %fusion.9 = (f32[4,256]{1,0:T(4,128)S(1)}, bf16[4,256,1024]{2,1,0:T(8,128)(2,1)}) fusion(bf16[4,256,1024]{2,1,0:T(8,128)(2,1)S(1)} %bitcast.53, bf16[4,256,768]{2,1,0:T(8,128)(2,1)S(1)} %multiply_convert_fusion.2, bf16[768,4,1024]{2,1,0:T(4,128)(2,1)} %param.11), kind=kOutput, calls=%fused_computation.13 | convolution fusion | flops 1615854592 | bytes 12062720 | tf_op jit(solution)/shard_map/erf,fed->erd/dot_general | solution.py:98
  83.7 10.8 %multiply_convert_fusion.1 = (bf16[4,256,768]{2,1,0:T(8,128)(2,1)S(1)}, bf16[4,256,768]{2,1,0:T(8,128)(2,1)S(1)}) fusion(f32[4,256,1536]{2,1,0:T(8,128)} %copy-done, bf16[4,256,1024]{2,1,0:T(8,128)(2,1)S(1)} %fusion.8, bf16[768,4,1024]{2,1,0:T(4,128)(2,1)} %param.11), kind=kOutput, calls=%fused_computation.19 | convolution fusion | flops 1620836352 | bytes 17825792 | tf_op jit(solution)/shard_map/erd,fed->erf/dot_general | solution.py:92
  97.3 2.7 %constant_dynamic-slice_fusion.4 = (bf16[4,256,256]{2,1,0:T(8,128)(2,1)S(1)}, bf16[4,256,256]{2,1,0:T(8,128)(2,1)S(1)}, bf16[4,256,256]{2,1,0:T(8,128)(2,1)}, bf16[4,256,256]{2,1,0:T(8,128)(2,1)}) fusion(bf16[4,256,1024]{2,1,0:T(8,128)(2,1)} %bitcast.56, s32[]{:T(128)S(6)} %select_n.65, s32[]{:T(128)S(6)} %select_n.64, s32[]{:T(128)S(6)} %select_n.63, ...), kind=kLoop, calls=%fused_computation.75 | loop fusion | bytes 4194320 | tf_op jit(solution)/shard_map/dynamic_slice | solution.py:57
  106.6 3.2 %all-to-all-start.2 = ((f32[4,4,128]{2,1,0:T(4,128)}), f32[4,4,128]{2,1,0:T(4,128)S(1)}, u32[]{:S(2)}, u32[]{:S(2)}) async-start(f32[4,4,128]{2,1,0:T(4,128)} %copy.70), calls=%async_computation.2 | async-start | bytes 16384 | tf_op jit(solution)/shard_map/all_to_all | solution.py:113
  118.0 4.7 %convolution_convert_fusion = bf16[4,256,1536]{2,1,0:T(8,128)(2,1)} fusion(bf16[4,256,1536]{2,1,0:T(8,128)(2,1)} %collective-permute-done.1, bf16[4,256,768]{2,1,0:T(8,128)(2,1)S(1)} %copy-done.10, bf16[4,256,768]{2,1,0:T(8,128)(2,1)S(1)} %copy-done.6, bf16[4,256,256]{1,2,0:T(8,128)(2,1)S(1)} %get-tuple-element.43, bf16[4,256,256]{1,2,0:T(8,128)(2,1)S(1)} %copy-done.13), kind=kOutput, calls=%fused_computation.15 | convolution fusion | flops 1633157120 | bytes 10485760 | tf_op jit(solution)/shard_map/era,erb->eab/dot_general | solution.py:73
  124.1 4.8 %all-to-all-start = ((bf16[4,128,1024]{2,1,0:T(8,128)(2,1)}), bf16[4,128,1024]{2,1,0:T(8,128)(2,1)S(1)}, u32[]{:S(2)}, u32[]{:S(2)}) async-start(bf16[4,128,1024]{2,1,0:T(8,128)(2,1)} %bitcast.7), calls=%async_computation | async-start | bytes 2097152 | tf_op jit(solution)/shard_map/all_to_all | solution.py:105
  128.9 10.4 %fusion.28 = bf16[4,256,1024]{2,1,0:T(8,128)(2,1)} fusion(bf16[1024,4,1536]{2,1,0:T(4,128)(2,1)} %param.10, bf16[4,256,768]{2,1,0:T(8,128)(2,1)} %copy-done.9, bf16[4,256,768]{2,1,0:T(8,128)(2,1)S(1)} %copy-done.7), kind=kOutput, calls=%fused_computation.35 | convolution fusion | flops 3228565504 | bytes 17825792 | tf_op jit(solution)/shard_map/erf,def->erd/dot_general | solution.py:99
  139.3 4.1 %fusion.32 = bf16[512,1024]{1,0:T(8,128)(2,1)} fusion(bf16[1024,1024]{1,0:T(8,128)(2,1)} %bitcast.67, pred[128,8,4,128]{3,2,1,0:T(4,128)(4,1)} %bitcast.60), kind=kOutput, calls=%fused_computation.37 | convolution fusion | flops 1074266112 | bytes 3670016 | tf_op jit(solution)/shard_map/ra,rd->ad/dot_general | solution.py:102
  145.6 9.2 %all-to-all-done = bf16[4,128,1024]{2,1,0:T(8,128)(2,1)S(1)} async-done(((bf16[4,128,1024]{2,1,0:T(8,128)(2,1)}), bf16[4,128,1024]{2,1,0:T(8,128)(2,1)S(1)}, u32[]{:S(2)}, u32[]{:S(2)}) %all-to-all-start) | async-done | bytes 1048608 | tf_op jit(solution)/shard_map/all_to_all | solution.py:105
  154.8 3.8 %all-to-all-start.1 = ((bf16[4,128,1024]{2,1,0:T(8,128)(2,1)}), bf16[4,128,1024]{2,1,0:T(8,128)(2,1)S(1)}, u32[]{:S(2)}, u32[]{:S(2)}) async-start(bf16[4,128,1024]{2,1,0:T(8,128)(2,1)} %bitcast.57), calls=%async_computation.1 | async-start | bytes 2097152 | tf_op jit(solution)/shard_map/all_to_all | solution.py:105
  158.6 4.6 %fusion.31 = bf16[4,192,1024]{2,1,0:T(8,128)(2,1)} fusion(bf16[4,256,1024]{2,1,0:T(8,128)(2,1)} %collective-permute-done.4, bf16[4,256,1024]{2,1,0:T(8,128)(2,1)} %copy-done.1, bf16[4,256,192]{2,1,0:T(8,128)(2,1)S(1)} %get-tuple-element.45, bf16[4,256,192]{2,1,0:T(8,128)(2,1)} %get-tuple-element.41), kind=kOutput, calls=%fused_computation.36 | convolution fusion | flops 816054272 | bytes 6553600 | tf_op jit(solution)/shard_map/era,erb->eab/dot_general | solution.py:73
  165.5 18.3 %all-to-all-done.1 = bf16[4,128,1024]{2,1,0:T(8,128)(2,1)S(1)} async-done(((bf16[4,128,1024]{2,1,0:T(8,128)(2,1)}), bf16[4,128,1024]{2,1,0:T(8,128)(2,1)S(1)}, u32[]{:S(2)}, u32[]{:S(2)}) %all-to-all-start.1) | async-done | bytes 1048608 | tf_op jit(solution)/shard_map/all_to_all | solution.py:105
  184.8 42.0 %collective-permute-done.5 = bf16[4,192,1024]{2,1,0:T(8,128)(2,1)} collective-permute-done((bf16[4,192,1024]{2,1,0:T(8,128)(2,1)}, bf16[4,192,1024]{2,1,0:T(8,128)(2,1)}, u32[]{:S(2)}, u32[]{:S(2)}) %collective-permute-start.5) | collective-permute-done | bytes 1572896 | tf_op jit(solution)/shard_map/ppermute | solution.py:79
  226.7 4.0 %add_bitcast_fusion.1 = f32[192,4,1024]{2,0,1:T(8,128)S(1)} fusion(bf16[4,192,1024]{2,1,0:T(8,128)(2,1)} %collective-permute-done.5, bf16[4,256,1024]{2,1,0:T(8,128)(2,1)} %collective-permute-done.4, bf16[4,256,1024]{2,1,0:T(8,128)(2,1)} %copy-done.1, bf16[4,256,192]{2,1,0:T(8,128)(2,1)} %get-tuple-element.44, bf16[4,256,192]{2,1,0:T(8,128)(2,1)} %get-tuple-element.38), kind=kOutput, calls=%fused_computation.17 | convolution fusion | flops 816840704 | bytes 9699328 | tf_op jit(solution)/shard_map/era,erb->eab/dot_general | solution.py:73
  230.8 3.7 %copy.78 = f32[192,4,1024]{2,1,0:T(4,128)} copy(f32[192,4,1024]{2,0,1:T(8,128)S(1)} %add_bitcast_fusion.1) | data formatting | bytes 6291456
  234.5 4.0 %add_bitcast_fusion = f32[256,4,1536]{2,0,1:T(8,128)S(1)} fusion(bf16[4,256,1536]{2,1,0:T(8,128)(2,1)} %collective-permute-done.2, bf16[4,256,1536]{2,1,0:T(8,128)(2,1)} %collective-permute-done.1, bf16[4,256,768]{2,1,0:T(8,128)(2,1)S(1)} %copy-done.11, bf16[4,256,768]{2,1,0:T(8,128)(2,1)S(1)} %copy-done.8, bf16[4,256,256]{1,2,0:T(8,128)(2,1)S(1)} %copy-done.14, ...), kind=kOutput, calls=%fused_computation.5 | convolution fusion | flops 1634729984 | bytes 16777216 | tf_op jit(solution)/shard_map/era,erb->eab/dot_general | solution.py:73
  238.5 6.7 %copy.77 = f32[256,4,1536]{2,1,0:T(4,128)} copy(f32[256,4,1536]{2,0,1:T(8,128)S(1)} %add_bitcast_fusion) | data formatting | bytes 12582912
  (78 shorter events, 33.0 us)
Async XLA Ops:
  7.2 33.4 %all-gather.7.cloned.1.call-start = ((), (), s32[]{:S(2)}) async-start(), calls=%async_computation.3 | async-start | bytes 1310720 | tf_op jit(solution)/shard_map/all_gather | solution.py:26
  7.9 61.6 %all-gather.9.cloned.1.call-start = ((), (), s32[]{:S(2)}) async-start(), calls=%async_computation.4 | async-start | bytes 1310720 | tf_op jit(solution)/shard_map/all_gather | solution.py:27
  37.3 32.2 %copy-start.12 = (pred[4,4,64,4,128]{4,3,2,1,0:T(4,128)(4,1)}, pred[4,4,64,4,128]{4,3,2,1,0:T(4,128)(4,1)S(1)}, u32[]{:S(2)}) copy-start(pred[4,4,64,4,128]{4,3,2,1,0:T(4,128)(4,1)S(1)} %broadcast_and_fusion) | copy-start | bytes 1572868
  43.0 9.9 %copy-start.4 = (bf16[1024,1024]{1,0:T(8,128)(2,1)}, bf16[1024,1024]{1,0:T(8,128)(2,1)S(1)}, u32[]{:S(2)}) copy-start(bf16[1024,1024]{1,0:T(8,128)(2,1)S(1)} %fusion.19) | copy-start | bytes 6291460
  72.0 9.1 %copy-start.2 = (bf16[1024,1024]{1,0:T(8,128)(2,1)}, bf16[1024,1024]{1,0:T(8,128)(2,1)S(1)}, u32[]{:S(2)}) copy-start(bf16[1024,1024]{1,0:T(8,128)(2,1)S(1)} %fusion.22) | copy-start | bytes 6291460
  83.7 10.8 %copy-start.1 = (bf16[4,256,1024]{2,1,0:T(8,128)(2,1)}, bf16[4,256,1024]{2,1,0:T(8,128)(2,1)S(1)}, u32[]{:S(2)}) copy-start(bf16[4,256,1024]{2,1,0:T(8,128)(2,1)S(1)} %fusion.8) | copy-start | bytes 6291460
  97.3 20.7 %collective-permute-start.1 = (bf16[4,256,1536]{2,1,0:T(8,128)(2,1)}, bf16[4,256,1536]{2,1,0:T(8,128)(2,1)}, u32[]{:S(2)}, u32[]{:S(2)}) collective-permute-start(bf16[4,256,1536]{2,1,0:T(8,128)(2,1)} %pad_maximum_fusion.2), channel_id=1, source_target_pairs={{0,1},{1,0},{2,3},{3,2},{4,5},{5,4},{6,7},{7,6},{8,9},{9,8},{10,11... | collective-permute-start | bytes 9437192 | tf_op jit(solution)/shard_map/ppermute | solution.py:52
  102.5 13.4 %collective-permute-start = (bf16[4,256,512]{1,2,0:T(8,128)(2,1)}, bf16[4,256,512]{1,2,0:T(8,128)(2,1)}, u32[]{:S(2)}, u32[]{:S(2)}) collective-permute-start(bf16[4,256,512]{1,2,0:T(8,128)(2,1)} %pad_maximum_fusion.13), channel_id=1, source_target_pairs={{0,1},{1,0},{2,3},{3,2},{4,5},{5,4},{6,7},{7,6},{8,9},{9,8},{10,11... | collective-permute-start | bytes 3145736 | tf_op jit(solution)/shard_map/ppermute | solution.py:52
  103.8 54.7 %collective-permute-start.4 = (bf16[4,256,1024]{2,1,0:T(8,128)(2,1)}, bf16[4,256,1024]{2,1,0:T(8,128)(2,1)}, u32[]{:S(2)}, u32[]{:S(2)}) collective-permute-start(bf16[4,256,1024]{2,1,0:T(8,128)(2,1)} %copy-done.1), channel_id=1, source_target_pairs={{0,1},{1,0},{2,3},{3,2},{4,5},{5,4},{6,7},{7,6},{8,9},{9,8},{10,11... | collective-permute-start | bytes 6291464 | tf_op jit(solution)/shard_map/ppermute | solution.py:52
  106.6 17.5 %all-to-all-start.2 = ((f32[4,4,128]{2,1,0:T(4,128)}), f32[4,4,128]{2,1,0:T(4,128)S(1)}, u32[]{:S(2)}, u32[]{:S(2)}) async-start(f32[4,4,128]{2,1,0:T(4,128)} %copy.70), calls=%async_computation.2 | async-start | bytes 16384 | tf_op jit(solution)/shard_map/all_to_all | solution.py:113
  109.9 3.8 %copy-start.3 = (bf16[4,256,1024]{2,1,0:T(8,128)(2,1)S(1)}, bf16[4,256,1024]{2,1,0:T(8,128)(2,1)}, u32[]{:S(2)}) copy-start(bf16[4,256,1024]{2,1,0:T(8,128)(2,1)} %get-tuple-element.47) | copy-start | bytes 6291460
  113.1 30.3 %collective-permute-start.3 = (bf16[4,256,384]{2,1,0:T(8,128)(2,1)}, bf16[4,256,384]{2,1,0:T(8,128)(2,1)}, u32[]{:S(2)}, u32[]{:S(2)}) collective-permute-start(bf16[4,256,384]{2,1,0:T(8,128)(2,1)} %pad_maximum_fusion.14), channel_id=1, source_target_pairs={{0,1},{1,0},{2,3},{3,2},{4,5},{5,4},{6,7},{7,6},{8,9},{9,8},{10,11... | collective-permute-start | bytes 2359304 | tf_op jit(solution)/shard_map/ppermute | solution.py:52
  113.6 4.4 %copy-start.6 = (bf16[4,256,768]{2,1,0:T(8,128)(2,1)S(1)}, bf16[4,256,768]{2,1,0:T(8,128)(2,1)}, u32[]{:S(2)}) copy-start(bf16[4,256,768]{2,1,0:T(8,128)(2,1)} %copy-done.5) | copy-start | bytes 4718596
  113.6 4.4 %copy-start.10 = (bf16[4,256,768]{2,1,0:T(8,128)(2,1)S(1)}, bf16[4,256,768]{2,1,0:T(8,128)(2,1)}, u32[]{:S(2)}) copy-start(bf16[4,256,768]{2,1,0:T(8,128)(2,1)} %copy-done.9) | copy-start | bytes 4718596
  113.6 4.4 %copy-start.13 = (bf16[4,256,256]{1,2,0:T(8,128)(2,1)S(1)}, bf16[4,256,256]{1,2,0:T(8,128)(2,1)}, u32[]{:S(2)}) copy-start(bf16[4,256,256]{1,2,0:T(8,128)(2,1)} %copy.81) | copy-start | bytes 1572868
  118.0 10.9 %copy-start.7 = (bf16[4,256,768]{2,1,0:T(8,128)(2,1)S(1)}, bf16[4,256,768]{2,1,0:T(8,128)(2,1)}, u32[]{:S(2)}) copy-start(bf16[4,256,768]{2,1,0:T(8,128)(2,1)} %copy-done.5) | copy-start | bytes 4718596
  122.7 111.8 %collective-permute-start.2 = (bf16[4,256,1536]{2,1,0:T(8,128)(2,1)}, bf16[4,256,1536]{2,1,0:T(8,128)(2,1)}, u32[]{:S(2)}, u32[]{:S(2)}) collective-permute-start(bf16[4,256,1536]{2,1,0:T(8,128)(2,1)} %convolution_convert_fusion), channel_id=1, source_target_pairs={{0,2},{1,3},{2,0},{3,1},{4,6},{5,7},{6,4},{7,5},{8,10},{9,11},{10,... | collective-permute-start | bytes 9437192 | tf_op jit(solution)/shard_map/ppermute | solution.py:79
  124.1 30.7 %all-to-all-start = ((bf16[4,128,1024]{2,1,0:T(8,128)(2,1)}), bf16[4,128,1024]{2,1,0:T(8,128)(2,1)S(1)}, u32[]{:S(2)}, u32[]{:S(2)}) async-start(bf16[4,128,1024]{2,1,0:T(8,128)(2,1)} %bitcast.7), calls=%async_computation | async-start | bytes 2097152 | tf_op jit(solution)/shard_map/all_to_all | solution.py:105
  154.8 29.0 %all-to-all-start.1 = ((bf16[4,128,1024]{2,1,0:T(8,128)(2,1)}), bf16[4,128,1024]{2,1,0:T(8,128)(2,1)S(1)}, u32[]{:S(2)}, u32[]{:S(2)}) async-start(bf16[4,128,1024]{2,1,0:T(8,128)(2,1)} %bitcast.57), calls=%async_computation.1 | async-start | bytes 2097152 | tf_op jit(solution)/shard_map/all_to_all | solution.py:105
  158.6 5.4 %copy-start.15 = (s32[128,6]{0,1:T(8,128)S(1)}, s32[128,6]{0,1:T(8,128)}, u32[]{:S(2)}) copy-start(s32[128,6]{0,1:T(8,128)} %param.7) | copy-start | bytes 9220
  163.2 63.5 %collective-permute-start.5 = (bf16[4,192,1024]{2,1,0:T(8,128)(2,1)}, bf16[4,192,1024]{2,1,0:T(8,128)(2,1)}, u32[]{:S(2)}, u32[]{:S(2)}) collective-permute-start(bf16[4,192,1024]{2,1,0:T(8,128)(2,1)} %fusion.31), channel_id=1, source_target_pairs={{0,2},{1,3},{2,0},{3,1},{4,6},{5,7},{6,4},{7,5},{8,10},{9,11},{10,... | collective-permute-start | bytes 4718600 | tf_op jit(solution)/shard_map/ppermute | solution.py:79
  230.8 3.7 %copy-start.8 = (bf16[4,256,768]{2,1,0:T(8,128)(2,1)S(1)}, bf16[4,256,768]{2,1,0:T(8,128)(2,1)}, u32[]{:S(2)}) copy-start(bf16[4,256,768]{2,1,0:T(8,128)(2,1)} %copy-done.5) | copy-start | bytes 4718596
  230.8 3.7 %copy-start.11 = (bf16[4,256,768]{2,1,0:T(8,128)(2,1)S(1)}, bf16[4,256,768]{2,1,0:T(8,128)(2,1)}, u32[]{:S(2)}) copy-start(bf16[4,256,768]{2,1,0:T(8,128)(2,1)} %copy-done.9) | copy-start | bytes 4718596
  230.8 3.7 %copy-start.14 = (bf16[4,256,256]{1,2,0:T(8,128)(2,1)S(1)}, bf16[4,256,256]{1,2,0:T(8,128)(2,1)}, u32[]{:S(2)}) copy-start(bf16[4,256,256]{1,2,0:T(8,128)(2,1)} %get-tuple-element.42) | copy-start | bytes 1572868
  (3 other events, 7.7 us)
Sparse Core Ops, SparseCore 0:
  9.5 30.9 all-gather.6
  42.1 27.3 all-gather.8

commit v2 on v1

--- a/solution.py
+++ b/solution.py
@@ -1,7 +1,9 @@
 import jax
 import jax.numpy as jnp
 from jax import lax
+from jax.experimental.layout import Layout, with_layout_constraint
 from jax.sharding import PartitionSpec as P
+
 
 CAP = 64
 CORES = 2
@@ -21,10 +23,21 @@
     first = lax.axis_index("expert") * local
     slots = sources * cap
 
-    all_ids = lax.all_gather(expert_ids.T, "expert", axis=0)
-    all_probs = lax.all_gather(gate_probs.T, "expert", axis=0)
-    all_tokens = lax.all_gather(tokens, "expert", axis=0, tiled=True)
-    all_cot = lax.all_gather(cotangent, "expert", axis=0, tiled=True)
+    def to_source(values, shift):
+        step = [(i, (i + shift) % sources) for i in range(sources)]
+        return lax.ppermute(values, "expert", step) if shift else values
+
+    notes = jnp.concatenate([expert_ids.T.astype(BF), gate_probs.T], axis=0)
+    flat = notes.reshape(-1)
+    extra = -(-flat.shape[0] // (16 * width)) * 16
+    flat = jnp.pad(flat, (0, extra * width - flat.shape[0])).reshape(extra, width)
+    packed = jnp.concatenate([tokens, flat], axis=0)
+    held = [to_source(packed, s) for s in range(sources)]
+    all_cot = jnp.concatenate([to_source(cotangent, s) for s in range(sources)], axis=0)
+    all_tokens = jnp.concatenate([h[:count] for h in held], axis=0)
+    all_notes = jnp.stack([h[count:].reshape(-1)[:notes.size].reshape(notes.shape) for h in held])
+    all_ids = all_notes[:, :top].astype(jnp.int32)
+    all_probs = all_notes[:, top:]
 
     named = (all_ids[None] == (first + jnp.arange(local, dtype=jnp.int32))[:, None, None, None])
     member = jnp.any(named, axis=2)
@@ -67,18 +80,27 @@
     def shared(values):
         return jnp.concatenate([values, swap(values)], axis=1)
 
-    def summed(left, right):
-        total = None
-        for shift in list(range(1, along)) + [0]:
-            part = jnp.einsum("era,erb->eab", left[shift], right, preferred_element_type=F32)
-            if shift:
-                step = [
-                    (x * CORES + c, ((x + shift) % along) * CORES + c)
-                    for x in range(along) for c in range(CORES)
-                ]
-                part = lax.ppermute(part.astype(BF), "replica", step).astype(F32)
-            total = part if total is None else total + part
-        return total.swapaxes(0, 1)
+    def part(left, right, shift):
+        return jnp.einsum("era,erb->eab", left[shift], right, preferred_element_type=F32)
+
+    def send_shares(left, right):
+        shares = []
+        for shift in range(1, along):
+            share = part(left, right, shift).astype(BF).swapaxes(0, 1)
+            share = with_layout_constraint(share, Layout((0, 1, 2)))
+            shares.append(share)
+        return shares
+
+    def total(left, right, shares):
+        own = with_layout_constraint(part(left, right, 0).swapaxes(0, 1), Layout((0, 1, 2)))
+        for shift in range(1, along):
+            step = [
+                (x * CORES + c, ((x + shift) % along) * CORES + c)
+                for x in range(along) for c in range(CORES)
+            ]
+            arrived = lax.ppermute(shares[shift - 1], "replica", step)
+            own = own + arrived.astype(F32)
+        return own
 
     input_columns = shared_columns(inputs)
     both_grad = shared(out_grad)
@@ -87,33 +109,49 @@
     gate, up = pre_act[..., :hidden_width], pre_act[..., hidden_width:]
     sig = jax.nn.sigmoid(gate)
     hidden = (gate * sig * up).astype(BF)
-    down_gradient = summed(shared_columns(hidden), both_grad)
+    hidden_columns = shared_columns(hidden)
+    outputs = jnp.einsum("erf,fed->erd", hidden, down_weights, preferred_element_type=F32).astype(BF)
+    down_shares = send_shares(hidden_columns, both_grad)
+    down_gradient = total(hidden_columns, both_grad, down_shares)
+    if down_shares:
+        later, _ = lax.optimization_barrier((out_grad, down_shares))
+    else:
+        later = out_grad
 
-    hidden_grad = jnp.einsum("erd,fed->erf", out_grad, down_weights, preferred_element_type=F32)
+    hidden_grad = jnp.einsum("erd,fed->erf", later, down_weights, preferred_element_type=F32)
     pre_grad = jnp.concatenate(
         [hidden_grad * up * sig * (1.0 + gate * (1.0 - sig)), hidden_grad * gate * sig], axis=-1
     ).astype(BF)
-    gate_up_gradient = summed(input_columns, shared(pre_grad))
-
-    outputs = jnp.einsum("erf,fed->erd", hidden, down_weights, preferred_element_type=F32).astype(BF)
-    input_grad = jnp.einsum("erf,def->erd", pre_grad, gate_up, preferred_element_type=F32).astype(BF)
+    both_pre = shared(pre_grad)
+    gate_shares = send_shares(input_columns, both_pre)
+    gate_up_gradient = total(input_columns, both_pre, gate_shares)
+    if gate_shares:
+        after, _ = lax.optimization_barrier((pre_grad, gate_shares))
+    else:
+        after = pre_grad
+    input_grad = jnp.einsum("erf,def->erd", after, gate_up, preferred_element_type=F32).astype(BF)
 
     def returned(matrix, values):
-        part = jnp.einsum(
+        parts = jnp.einsum(
             "ra,rd->ad", matrix, values.reshape(local * slots, width), preferred_element_type=F32
         ).astype(BF).reshape(sources, count, width)
-        arrived = lax.all_to_all(part, "expert", split_axis=0, concat_axis=0, tiled=True)
-        return jnp.sum(arrived.astype(F32), axis=0).astype(BF)
+        arrived = [to_source(parts[s], -s).astype(F32) for s in range(sources)]
+        return sum(arrived[1:], arrived[0]).astype(BF)
 
     combined = returned(back, outputs)
     token_gradient = returned(pick, input_grad)
 
     slot_prob = jnp.sum(raw_cot.astype(F32) * outputs.astype(F32), axis=2).reshape(local, sources, cap, 1)
     prob_part = jnp.sum(jnp.where(chosen, slot_prob, 0.0), axis=2).swapaxes(0, 1)
-    prob_all = lax.all_to_all(prob_part, "expert", split_axis=0, concat_axis=0, tiled=True)
-    prob_all = prob_all.reshape(sources * local, count)
-    mine = expert_ids.T[:, None, :] == jnp.arange(sources * local, dtype=jnp.int32)[None, :, None]
-    prob_gradient = jnp.sum(jnp.where(mine, prob_all[None], 0.0), axis=1).T
+    choice = expert_ids.T
+    prob_gradient = jnp.zeros((top, count), F32)
+    home = lax.axis_index("expert")
+    for s in range(sources):
+        block = lax.rem(home + s, sources) * local
+        theirs = to_source(prob_part[s], -s)
+        hit = choice[:, None, :] == (block + jnp.arange(local, dtype=jnp.int32))[None, :, None]
+        prob_gradient = prob_gradient + jnp.sum(jnp.where(hit, theirs[None], 0.0), axis=1)
+    prob_gradient = prob_gradient.T
     return (combined, token_gradient, prob_gradient, gate_up_gradient, down_gradient)
 
 

time: 257 us -> 261 us (1.016)
  blocking collectives: 27.4 us -> 0 us
  starting transfers between devices: 14.9 us -> 36.8 us
  other arithmetic: 12.1 us -> 28 us
  between operations: 14.8 us -> 1.4 us
  waiting for transfers between devices: 87.1 us -> 99.3 us
  local copies, waits for them, and re-layouts: 27.3 us -> 24.3 us
    ppermute x2 -> x17, waiting for transfers between devices: 42 us -> 96.5 us  [the longest x15 68.3 us: to_source(): return lax.ppermute(values, 'expert', step) if shift else values]
    ppermute x2 -> x17, starting transfers between devices: 2.02 us -> 35.9 us  [the longest x15 32.8 us: to_source(): return lax.ppermute(values, 'expert', step) if shift else values]
    all_to_all x3 -> x0, waiting for transfers between devices: 27.5 us -> none  [the longest x2 27.5 us: returned(): lax.all_to_all(part, 'expert', split_axis=0, concat_axis=0, tiled=True)]
    all_gather x2 -> x0, blocking collectives: 27.4 us -> none  [the longest x1 13.8 us: on_device(): all_probs = lax.all_gather(gate_probs.T, 'expert', axis=0)]
    all_gather x2 -> x0, waiting for transfers between devices: 16.2 us -> none  [the longest x1 12.9 us: on_device(): all_cot = lax.all_gather(cotangent, 'expert', axis=0, tiled=True)]
    add x0 -> x5, other arithmetic: none -> 14.2 us  [the longest x2 13.6 us: total(): own = own + arrived.astype(F32)]
    all_to_all x3 -> x0, starting transfers between devices: 11.8 us -> none  [the longest x2 8.52 us: returned(): lax.all_to_all(part, 'expert', split_axis=0, concat_axis=0, tiled=True)]
    dot_general x1, matrix products: 9.08 us -> 4.05 us  [on_device(): jnp.einsum('erf,fed->erd', hidden, down_weights, preferred_element_type=F32)]
  transfers between devices with their start and end apart: 11 -> 21, of which waited for: 5 -> 11; matrix products, arithmetic and copies ran while one was open for 27% -> 27% of each run, Pallas kernels for 0% -> 0%
where the time goes in v2:
time: 261 us; the launch traced here: 256 us
  waiting for transfers between devices  99.3 us (38%)
  matrix products  66.4 us (25%)
  starting transfers between devices  36.8 us (14%)
  other arithmetic  28 us (11%)
  local copies, waits for them, and re-layouts  24.3 us (9%)
    ppermute x15, waiting for transfers between devices, to_source(): return lax.ppermute(values, 'expert', step) if shift else values  68.3 us
    ppermute x15, starting transfers between devices, to_source(): return lax.ppermute(values, 'expert', step) if shift else values  32.8 us
    ppermute x2, waiting for transfers between devices, total(): arrived = lax.ppermute(shares[shift - 1], 'replica', step)  28.2 us
    dot_general x1, matrix products, on_device(): jnp.einsum('erd,fed->erf', later, down_weights, preferred_element_type=F32)  17.7 us
    unnamed x69, local copies, waits for them, and re-layouts  16.8 us
    dot_general x4, matrix products, part(): jnp.einsum('era,erb->eab', left[shift], right, preferred_element_type=F32)  14.5 us
    add x2, other arithmetic, total(): own = own + arrived.astype(F32)  13.6 us
    dot_general x1, matrix products, on_device(): jnp.einsum('erf,def->erd', after, gate_up, preferred_element_type=F32)  11.3 us
  transfers between devices with their start and end apart: 21, of which 11 were waited for; matrix products, arithmetic and copies ran while one was open for 27% of the time, Pallas kernels for 0%

profile of v2, /device:TPU:0, one launch (start us, length us, event | category | flops | bytes accessed | tf_op | source)
XLA Modules:
  0.0 256.1 jit_solution(4475474268694053946)
XLA Ops:
  3.1 5.1 %collective-permute-start.2 = (bf16[144,1024]{1,0:T(8,128)(2,1)S(1)}, bf16[144,1024]{1,0:T(8,128)(2,1)S(1)}, u32[]{:S(2)}, u32[]{:S(2)}) collective-permute-start(bf16[144,1024]{1,0:T(8,128)(2,1)S(1)} %constant_dynamic-update-slice_fusion), channel_id=1, source_target_pairs={{0,12},{4,0},{8,4},{12,8},{1,13},{5,1},{9,5},{13,9},{2,14},{6,2},{... | collective-permute-start | bytes 884744 | tf_op jit(solution)/shard_map/ppermute | solution.py:28
  15.7 10.6 %collective-permute-start = (bf16[144,1024]{1,0:T(8,128)(2,1)S(1)}, bf16[144,1024]{1,0:T(8,128)(2,1)S(1)}, u32[]{:S(2)}, u32[]{:S(2)}) collective-permute-start(bf16[144,1024]{1,0:T(8,128)(2,1)S(1)} %constant_dynamic-update-slice_fusion), channel_id=1, source_target_pairs={{0,4},{4,8},{8,12},{12,0},{1,5},{5,9},{9,13},{13,1},{2,6},{6,10},{... | collective-permute-start | bytes 884744 | tf_op jit(solution)/shard_map/ppermute | solution.py:28
  26.3 29.6 %collective-permute-done.1 = bf16[144,1024]{1,0:T(8,128)(2,1)S(1)} collective-permute-done((bf16[144,1024]{1,0:T(8,128)(2,1)S(1)}, bf16[144,1024]{1,0:T(8,128)(2,1)S(1)}, u32[]{:S(2)}, u32[]{:S(2)}) %collective-permute-start.1) | collective-permute-done | bytes 294944 | tf_op jit(solution)/shard_map/ppermute | solution.py:28
  58.4 10.2 %fusion.2 = f32[4,256,1536]{2,1,0:T(8,128)S(1)} fusion(bf16[4,256,1024]{2,1,0:T(8,128)(2,1)S(1)} %bitcast.81, bf16[1024,4,1536]{2,1,0:T(4,128)(2,1)} %param.10), kind=kOutput, calls=%fused_computation.2 | convolution fusion | flops 3221225472 | bytes 20971520 | tf_op jit(solution)/shard_map/erd,def->erf/dot_general | solution.py:108
  71.2 4.0 %fusion.25 = bf16[4,256,1024]{2,1,0:T(8,128)(2,1)S(1)} fusion(bf16[4,256,768]{2,1,0:T(8,128)(2,1)S(1)} %multiply_convert_fusion.2, bf16[768,4,1024]{2,1,0:T(4,128)(2,1)S(1)} %bitcast.98), kind=kOutput, calls=%fused_computation.35 | convolution fusion | flops 1611661312 | bytes 9961472 | tf_op jit(solution)/shard_map/erf,fed->erd/dot_general | solution.py:113
  75.5 2.9 %fusion.22 = bf16[1024,1024]{1,0:T(8,128)(2,1)S(1)} fusion(pred[128,8,4,128]{3,2,1,0:T(4,128)(4,1)S(1)} %bitcast.85, bf16[128,1024]{1,0:T(8,128)(2,1)} %collective-permute-done.8, bf16[128,1024]{1,0:T(8,128)(2,1)} %collective-permute-done.7, bf16[128,1024]{1,0:T(8,128)(2,1)} %collective-permute-done.6, bf16[128,1024]{1,0:T(8,128)(2,1)S(1)} %copy-done.21), kind=kOutput, calls=%fused_computation.34 | convolution fusion | flops 1078984704 | bytes 3670016 | tf_op jit(solution)/shard_map/dot_general | solution.py:56
  81.0 3.4 %fusion.8 = bf16[4,256,1024]{2,1,0:T(8,128)(2,1)} fusion(f32[4,256]{1,0:T(4,128)S(1)} %mul.91, bf16[1024,1024]{1,0:T(8,128)(2,1)} %copy-done), kind=kLoop, calls=%fused_computation.12 | loop fusion | flops 3145728 | bytes 4198400 | tf_op jit(solution)/shard_map/convert_element_type | solution.py:60
  90.9 3.9 %fusion.31 = bf16[4,192,1024]{2,1,0:T(8,128)(2,1)S(1)} fusion(bf16[4,256,1024]{2,1,0:T(8,128)(2,1)} %collective-permute-done.10, bf16[4,256,1024]{2,1,0:T(8,128)(2,1)} %fusion.8, bf16[4,256,192]{2,1,0:T(8,128)(2,1)S(1)} %get-tuple-element.34, bf16[4,256,192]{2,1,0:T(8,128)(2,1)S(1)} %get-tuple-element.24), kind=kOutput, calls=%fused_computation.37 | convolution fusion | flops 816054272 | bytes 6553600 | tf_op jit(solution)/shard_map/era,erb->eab/dot_general | solution.py:84
  97.3 17.7 %multiply_convert_fusion.1 = (bf16[4,256,768]{2,1,0:T(8,128)(2,1)S(1)}, bf16[4,256,768]{2,1,0:T(8,128)(2,1)S(1)}) fusion(f32[4,256,1536]{2,1,0:T(8,128)S(1)} %bitcast.78, bf16[4,256,1024]{2,1,0:T(8,128)(2,1)} %fusion.8, bf16[768,4,1024]{2,1,0:T(4,128)(2,1)S(1)} %bitcast.100), kind=kOutput, calls=%fused_computation.20 | convolution fusion | flops 1620836352 | bytes 17825792 | tf_op jit(solution)/shard_map/erd,fed->erf/dot_general | solution.py:121
  128.6 3.0 %collective-permute-start.17 = (f32[4,128]{1,0:T(4,128)S(1)}, f32[4,128]{1,0:T(4,128)S(1)}, u32[]{:S(2)}, u32[]{:S(2)}) collective-permute-start(f32[4,128]{1,0:T(4,128)S(1)} %bitcast.95), channel_id=1, source_target_pairs={{0,8},{4,12},{8,0},{12,4},{1,9},{5,13},{9,1},{13,5},{2,10},{6,14},... | collective-permute-start | bytes 6152 | tf_op jit(solution)/shard_map/ppermute | solution.py:28
  131.6 6.2 %collective-permute-done.18 = f32[4,128]{1,0:T(4,128)S(1)} collective-permute-done((f32[4,128]{1,0:T(4,128)S(1)}, f32[4,128]{1,0:T(4,128)S(1)}, u32[]{:S(2)}, u32[]{:S(2)}) %collective-permute-start.18) | collective-permute-done | bytes 2080 | tf_op jit(solution)/shard_map/ppermute | solution.py:28
  146.3 7.0 %collective-permute-done.5 = bf16[128,1024]{1,0:T(8,128)(2,1)S(1)} collective-permute-done((bf16[128,1024]{1,0:T(8,128)(2,1)}, bf16[128,1024]{1,0:T(8,128)(2,1)S(1)}, u32[]{:S(2)}, u32[]{:S(2)}) %collective-permute-start.5) | collective-permute-done | bytes 262176 | tf_op jit(solution)/shard_map/ppermute | solution.py:28
  153.3 9.3 %collective-permute-done.4 = bf16[128,1024]{1,0:T(8,128)(2,1)S(1)} collective-permute-done((bf16[128,1024]{1,0:T(8,128)(2,1)S(1)}, bf16[128,1024]{1,0:T(8,128)(2,1)S(1)}, u32[]{:S(2)}, u32[]{:S(2)}) %collective-permute-start.4) | collective-permute-done | bytes 262176 | tf_op jit(solution)/shard_map/ppermute | solution.py:28
  165.5 3.9 %convolution_convert_fusion = bf16[4,256,1536]{2,1,0:T(8,128)(2,1)S(1)} fusion(bf16[4,256,1536]{2,1,0:T(8,128)(2,1)} %collective-permute-done.12, bf16[4,256,768]{2,1,0:T(8,128)(2,1)S(1)} %copy-done.11, bf16[4,256,768]{2,1,0:T(8,128)(2,1)S(1)} %copy-done.8, bf16[4,256,256]{1,2,0:T(8,128)(2,1)S(1)} %get-tuple-element.26, bf16[4,256,256]{1,2,0:T(8,128)(2,1)} %copy.43), kind=kOutput, calls=%fused_computation.15 | convolution fusion | flops 1633157120 | bytes 10485760 | tf_op jit(solution)/shard_map/era,erb->eab/dot_general | solution.py:84
  173.4 3.2 %fusion.10 = f32[4,192,1024]{2,1,0:T(8,128)S(1)} fusion(bf16[4,256,1024]{2,1,0:T(8,128)(2,1)} %collective-permute-done.10, bf16[4,256,1024]{2,1,0:T(8,128)(2,1)} %fusion.8, bf16[4,256,192]{2,1,0:T(8,128)(2,1)S(1)} %copy-done.16, bf16[4,256,192]{2,1,0:T(8,128)(2,1)S(1)} %copy-done.18), kind=kOutput, calls=%fused_computation.23 | convolution fusion | flops 815267840 | bytes 8126464 | tf_op jit(solution)/shard_map/era,erb->eab/dot_general | solution.py:84
  176.6 4.7 %collective-permute-done.20 = bf16[192,4,1024]{2,1,0:T(4,128)(2,1)S(1)} collective-permute-done((bf16[192,4,1024]{2,1,0:T(4,128)(2,1)S(1)}, bf16[192,4,1024]{2,1,0:T(4,128)(2,1)S(1)}, u32[]{:S(2)}, u32[]{:S(2)}) %collective-permute-start.20) | collective-permute-done | bytes 1572896 | tf_op jit(solution)/shard_map/ppermute | solution.py:101
  181.3 4.1 %bitcast_add_fusion.1 = f32[192,4,1024]{2,1,0:T(4,128)} fusion(f32[4,192,1024]{2,1,0:T(8,128)S(1)} %fusion.10, bf16[192,4,1024]{2,1,0:T(4,128)(2,1)S(1)} %collective-permute-done.20), kind=kLoop, calls=%fused_computation.18 | loop fusion | flops 1572864 | bytes 7864320 | tf_op jit(solution)/shard_map/add | solution.py:102
  185.5 11.3 %fusion.28 = bf16[4,256,1024]{2,1,0:T(8,128)(2,1)} fusion(bf16[4,256,1536]{2,1,0:T(8,128)(2,1)} %pad_maximum_fusion.2, bf16[1024,4,1536]{2,1,0:T(4,128)(2,1)} %param.10), kind=kOutput, calls=%fused_computation.36 | convolution fusion | flops 3222274048 | bytes 17825792 | tf_op jit(solution)/shard_map/erf,def->erd/dot_general | solution.py:132
  196.8 3.0 %fusion.32 = bf16[512,1024]{1,0:T(8,128)(2,1)S(1)} fusion(bf16[1024,1024]{1,0:T(8,128)(2,1)} %bitcast.101, pred[128,8,4,128]{3,2,1,0:T(4,128)(4,1)S(1)} %bitcast.86), kind=kOutput, calls=%fused_computation.39 | convolution fusion | flops 1074266112 | bytes 3670016 | tf_op jit(solution)/shard_map/ra,rd->ad/dot_general | solution.py:135
  204.9 3.4 %fusion.12 = f32[4,256,1536]{2,1,0:T(8,128)S(1)} fusion(bf16[4,256,1536]{2,1,0:T(8,128)(2,1)} %collective-permute-done.12, bf16[4,256,768]{2,1,0:T(8,128)(2,1)S(1)} %copy-done.12, bf16[4,256,768]{2,1,0:T(8,128)(2,1)S(1)} %copy-done.9, bf16[4,256,256]{1,2,0:T(8,128)(2,1)S(1)} %copy-done.17, bf16[4,256,256]{1,2,0:T(8,128)(2,1)S(1)} %copy-done.15), kind=kOutput, calls=%fused_computation.25 | convolution fusion | flops 1631584256 | bytes 13631488 | tf_op jit(solution)/shard_map/era,erb->eab/dot_general | solution.py:84
  209.1 4.7 %collective-permute-done.15 = bf16[128,1024]{1,0:T(8,128)(2,1)S(1)} collective-permute-done((bf16[128,1024]{1,0:T(8,128)(2,1)S(1)}, bf16[128,1024]{1,0:T(8,128)(2,1)S(1)}, u32[]{:S(2)}, u32[]{:S(2)}) %collective-permute-start.15) | collective-permute-done | bytes 262176 | tf_op jit(solution)/shard_map/ppermute | solution.py:28
  213.8 8.2 %collective-permute-done.14 = bf16[128,1024]{1,0:T(8,128)(2,1)S(1)} collective-permute-done((bf16[128,1024]{1,0:T(8,128)(2,1)S(1)}, bf16[128,1024]{1,0:T(8,128)(2,1)S(1)}, u32[]{:S(2)}, u32[]{:S(2)}) %collective-permute-start.14) | collective-permute-done | bytes 262176 | tf_op jit(solution)/shard_map/ppermute | solution.py:28
  223.0 23.5 %collective-permute-done.19 = bf16[256,4,1536]{2,1,0:T(4,128)(2,1)} collective-permute-done((bf16[256,4,1536]{2,1,0:T(4,128)(2,1)S(1)}, bf16[256,4,1536]{2,1,0:T(4,128)(2,1)}, u32[]{:S(2)}, u32[]{:S(2)}) %collective-permute-start.19) | collective-permute-done | bytes 3145760 | tf_op jit(solution)/shard_map/ppermute | solution.py:101
  246.5 9.4 %bitcast_add_fusion = f32[256,4,1536]{2,1,0:T(4,128)} fusion(f32[4,256,1536]{2,1,0:T(8,128)S(1)} %fusion.12, bf16[256,4,1536]{2,1,0:T(4,128)(2,1)} %collective-permute-done.19), kind=kLoop, calls=%fused_computation.5 | loop fusion | flops 3145728 | bytes 15728640 | tf_op jit(solution)/shard_map/add | solution.py:102
  (148 shorter events, 62.1 us)
Async XLA Ops:
  0.6 56.4 %copy-start.19 = (bf16[128,1024]{1,0:T(8,128)(2,1)S(1)}, bf16[128,1024]{1,0:T(8,128)(2,1)}, u32[]{:S(2)}) copy-start(bf16[128,1024]{1,0:T(8,128)(2,1)} %param.6) | copy-start | bytes 786436
  3.1 12.6 %collective-permute-start.2 = (bf16[144,1024]{1,0:T(8,128)(2,1)S(1)}, bf16[144,1024]{1,0:T(8,128)(2,1)S(1)}, u32[]{:S(2)}, u32[]{:S(2)}) collective-permute-start(bf16[144,1024]{1,0:T(8,128)(2,1)S(1)} %constant_dynamic-update-slice_fusion), channel_id=1, source_target_pairs={{0,12},{4,0},{8,4},{12,8},{1,13},{5,1},{9,5},{13,9},{2,14},{6,2},{... | collective-permute-start | bytes 884744 | tf_op jit(solution)/shard_map/ppermute | solution.py:28
  8.2 67.2 %collective-permute-start.7 = (bf16[128,1024]{1,0:T(8,128)(2,1)}, bf16[128,1024]{1,0:T(8,128)(2,1)}, u32[]{:S(2)}, u32[]{:S(2)}) collective-permute-start(bf16[128,1024]{1,0:T(8,128)(2,1)} %param.9), channel_id=1, source_target_pairs={{0,8},{4,12},{8,0},{12,4},{1,9},{5,13},{9,1},{13,5},{2,10},{6,14},... | collective-permute-start | bytes 786440 | tf_op jit(solution)/shard_map/ppermute | solution.py:28
  8.2 67.2 %collective-permute-start.6 = (bf16[128,1024]{1,0:T(8,128)(2,1)}, bf16[128,1024]{1,0:T(8,128)(2,1)}, u32[]{:S(2)}, u32[]{:S(2)}) collective-permute-start(bf16[128,1024]{1,0:T(8,128)(2,1)} %param.9), channel_id=1, source_target_pairs={{0,4},{4,8},{8,12},{12,0},{1,5},{5,9},{9,13},{13,1},{2,6},{6,10},{... | collective-permute-start | bytes 786440 | tf_op jit(solution)/shard_map/ppermute | solution.py:28
  9.2 66.2 %collective-permute-start.8 = (bf16[128,1024]{1,0:T(8,128)(2,1)}, bf16[128,1024]{1,0:T(8,128)(2,1)}, u32[]{:S(2)}, u32[]{:S(2)}) collective-permute-start(bf16[128,1024]{1,0:T(8,128)(2,1)} %param.9), channel_id=1, source_target_pairs={{0,12},{4,0},{8,4},{12,8},{1,13},{5,1},{9,5},{13,9},{2,14},{6,2},{... | collective-permute-start | bytes 786440 | tf_op jit(solution)/shard_map/ppermute | solution.py:28
  12.0 43.8 %collective-permute-start.1 = (bf16[144,1024]{1,0:T(8,128)(2,1)S(1)}, bf16[144,1024]{1,0:T(8,128)(2,1)S(1)}, u32[]{:S(2)}, u32[]{:S(2)}) collective-permute-start(bf16[144,1024]{1,0:T(8,128)(2,1)S(1)} %constant_dynamic-update-slice_fusion), channel_id=1, source_target_pairs={{0,8},{4,12},{8,0},{12,4},{1,9},{5,13},{9,1},{13,5},{2,10},{6,14},... | collective-permute-start | bytes 884744 | tf_op jit(solution)/shard_map/ppermute | solution.py:28
  15.7 40.2 %collective-permute-start = (bf16[144,1024]{1,0:T(8,128)(2,1)S(1)}, bf16[144,1024]{1,0:T(8,128)(2,1)S(1)}, u32[]{:S(2)}, u32[]{:S(2)}) collective-permute-start(bf16[144,1024]{1,0:T(8,128)(2,1)S(1)} %constant_dynamic-update-slice_fusion), channel_id=1, source_target_pairs={{0,4},{4,8},{8,12},{12,0},{1,5},{5,9},{9,13},{13,1},{2,6},{6,10},{... | collective-permute-start | bytes 884744 | tf_op jit(solution)/shard_map/ppermute | solution.py:28
  84.4 6.5 %collective-permute-start.10 = (bf16[4,256,1024]{2,1,0:T(8,128)(2,1)}, bf16[4,256,1024]{2,1,0:T(8,128)(2,1)}, u32[]{:S(2)}, u32[]{:S(2)}) collective-permute-start(bf16[4,256,1024]{2,1,0:T(8,128)(2,1)} %fusion.8), channel_id=1, source_target_pairs={{0,1},{1,0},{2,3},{3,2},{4,5},{5,4},{6,7},{7,6},{8,9},{9,8},{10,11... | collective-permute-start | bytes 6291464 | tf_op jit(solution)/shard_map/ppermute | solution.py:65
  86.5 3.4 %collective-permute-start.9 = (bf16[4,256,384]{2,1,0:T(8,128)(2,1)S(1)}, bf16[4,256,384]{2,1,0:T(8,128)(2,1)S(1)}, u32[]{:S(2)}, u32[]{:S(2)}) collective-permute-start(bf16[4,256,384]{2,1,0:T(8,128)(2,1)S(1)} %pad_maximum_fusion.10), channel_id=1, source_target_pairs={{0,1},{1,0},{2,3},{3,2},{4,5},{5,4},{6,7},{7,6},{8,9},{9,8},{10,11... | collective-permute-start | bytes 2359304 | tf_op jit(solution)/shard_map/ppermute | solution.py:65
  117.8 47.7 %collective-permute-start.12 = (bf16[4,256,1536]{2,1,0:T(8,128)(2,1)}, bf16[4,256,1536]{2,1,0:T(8,128)(2,1)}, u32[]{:S(2)}, u32[]{:S(2)}) collective-permute-start(bf16[4,256,1536]{2,1,0:T(8,128)(2,1)} %pad_maximum_fusion.2), channel_id=1, source_target_pairs={{0,1},{1,0},{2,3},{3,2},{4,5},{5,4},{6,7},{7,6},{8,9},{9,8},{10,11... | collective-permute-start | bytes 9437192 | tf_op jit(solution)/shard_map/ppermute | solution.py:65
  123.3 40.1 %collective-permute-start.11 = (bf16[4,256,512]{1,2,0:T(8,128)(2,1)}, bf16[4,256,512]{1,2,0:T(8,128)(2,1)}, u32[]{:S(2)}, u32[]{:S(2)}) collective-permute-start(bf16[4,256,512]{1,2,0:T(8,128)(2,1)} %pad_maximum_fusion.9), channel_id=1, source_target_pairs={{0,1},{1,0},{2,3},{3,2},{4,5},{5,4},{6,7},{7,6},{8,9},{9,8},{10,11... | collective-permute-start | bytes 3145736 | tf_op jit(solution)/shard_map/ppermute | solution.py:65
  126.5 17.5 %collective-permute-start.3 = (bf16[128,1024]{1,0:T(8,128)(2,1)}, bf16[128,1024]{1,0:T(8,128)(2,1)S(1)}, u32[]{:S(2)}, u32[]{:S(2)}) collective-permute-start(bf16[128,1024]{1,0:T(8,128)(2,1)} %get-tuple-element.30), channel_id=1, source_target_pairs={{0,12},{4,0},{8,4},{12,8},{1,13},{5,1},{9,5},{13,9},{2,14},{6,2},{... | collective-permute-start | bytes 786440 | tf_op jit(solution)/shard_map/ppermute | solution.py:28
  126.6 11.3 %collective-permute-start.18 = (f32[4,128]{1,0:T(4,128)S(1)}, f32[4,128]{1,0:T(4,128)S(1)}, u32[]{:S(2)}, u32[]{:S(2)}) collective-permute-start(f32[4,128]{1,0:T(4,128)S(1)} %bitcast.96), channel_id=1, source_target_pairs={{0,4},{4,8},{8,12},{12,0},{1,5},{5,9},{9,13},{13,1},{2,6},{6,10},{... | collective-permute-start | bytes 6152 | tf_op jit(solution)/shard_map/ppermute | solution.py:28
  128.6 13.3 %collective-permute-start.17 = (f32[4,128]{1,0:T(4,128)S(1)}, f32[4,128]{1,0:T(4,128)S(1)}, u32[]{:S(2)}, u32[]{:S(2)}) collective-permute-start(f32[4,128]{1,0:T(4,128)S(1)} %bitcast.95), channel_id=1, source_target_pairs={{0,8},{4,12},{8,0},{12,4},{1,9},{5,13},{9,1},{13,5},{2,10},{6,14},... | collective-permute-start | bytes 6152 | tf_op jit(solution)/shard_map/ppermute | solution.py:28
  137.8 6.2 %collective-permute-start.16 = (f32[4,128]{1,0:T(4,128)S(1)}, f32[4,128]{1,0:T(4,128)S(1)}, u32[]{:S(2)}, u32[]{:S(2)}) collective-permute-start(f32[4,128]{1,0:T(4,128)S(1)} %bitcast.94), channel_id=1, source_target_pairs={{0,12},{4,0},{8,4},{12,8},{1,13},{5,1},{9,5},{13,9},{2,14},{6,2},{... | collective-permute-start | bytes 6152 | tf_op jit(solution)/shard_map/ppermute | solution.py:28
  141.9 23.6 %copy-start.8 = (bf16[4,256,768]{2,1,0:T(8,128)(2,1)S(1)}, bf16[4,256,768]{2,1,0:T(8,128)(2,1)}, u32[]{:S(2)}) copy-start(bf16[4,256,768]{2,1,0:T(8,128)(2,1)} %copy-done.7) | copy-start | bytes 4718596
  141.9 23.6 %copy-start.11 = (bf16[4,256,768]{2,1,0:T(8,128)(2,1)S(1)}, bf16[4,256,768]{2,1,0:T(8,128)(2,1)}, u32[]{:S(2)}) copy-start(bf16[4,256,768]{2,1,0:T(8,128)(2,1)} %copy-done.10) | copy-start | bytes 4718596
  141.9 11.3 %collective-permute-start.5 = (bf16[128,1024]{1,0:T(8,128)(2,1)}, bf16[128,1024]{1,0:T(8,128)(2,1)S(1)}, u32[]{:S(2)}, u32[]{:S(2)}) collective-permute-start(bf16[128,1024]{1,0:T(8,128)(2,1)} %get-tuple-element.31), channel_id=1, source_target_pairs={{0,4},{4,8},{8,12},{12,0},{1,5},{5,9},{9,13},{13,1},{2,6},{6,10},{... | collective-permute-start | bytes 786440 | tf_op jit(solution)/shard_map/ppermute | solution.py:28
  144.0 18.6 %collective-permute-start.4 = (bf16[128,1024]{1,0:T(8,128)(2,1)S(1)}, bf16[128,1024]{1,0:T(8,128)(2,1)S(1)}, u32[]{:S(2)}, u32[]{:S(2)}) collective-permute-start(bf16[128,1024]{1,0:T(8,128)(2,1)S(1)} %get-tuple-element.32), channel_id=1, source_target_pairs={{0,8},{4,12},{8,0},{12,4},{1,9},{5,13},{9,1},{13,5},{2,10},{6,14},... | collective-permute-start | bytes 786440 | tf_op jit(solution)/shard_map/ppermute | solution.py:28
  144.0 37.3 %collective-permute-start.20 = (bf16[192,4,1024]{2,1,0:T(4,128)(2,1)S(1)}, bf16[192,4,1024]{2,1,0:T(4,128)(2,1)S(1)}, u32[]{:S(2)}, u32[]{:S(2)}) collective-permute-start(bf16[192,4,1024]{2,1,0:T(4,128)(2,1)S(1)} %bitcast.83), channel_id=1, source_target_pairs={{0,2},{1,3},{2,0},{3,1},{4,6},{5,7},{6,4},{7,5},{8,10},{9,11},{10,... | collective-permute-start | bytes 4718600 | tf_op jit(solution)/shard_map/ppermute | solution.py:101
  171.8 74.6 %collective-permute-start.19 = (bf16[256,4,1536]{2,1,0:T(4,128)(2,1)S(1)}, bf16[256,4,1536]{2,1,0:T(4,128)(2,1)}, u32[]{:S(2)}, u32[]{:S(2)}) collective-permute-start(bf16[256,4,1536]{2,1,0:T(4,128)(2,1)S(1)} %bitcast.80), channel_id=1, source_target_pairs={{0,2},{1,3},{2,0},{3,1},{4,6},{5,7},{6,4},{7,5},{8,10},{9,11},{10,... | collective-permute-start | bytes 9437192 | tf_op jit(solution)/shard_map/ppermute | solution.py:101
  199.9 9.2 %collective-permute-start.13 = (bf16[128,1024]{1,0:T(8,128)(2,1)S(1)}, bf16[128,1024]{1,0:T(8,128)(2,1)S(1)}, u32[]{:S(2)}, u32[]{:S(2)}) collective-permute-start(bf16[128,1024]{1,0:T(8,128)(2,1)S(1)} %get-tuple-element.27), channel_id=1, source_target_pairs={{0,12},{4,0},{8,4},{12,8},{1,13},{5,1},{9,5},{13,9},{2,14},{6,2},{... | collective-permute-start | bytes 786440 | tf_op jit(solution)/shard_map/ppermute | solution.py:28
  202.4 11.5 %collective-permute-start.15 = (bf16[128,1024]{1,0:T(8,128)(2,1)S(1)}, bf16[128,1024]{1,0:T(8,128)(2,1)S(1)}, u32[]{:S(2)}, u32[]{:S(2)}) collective-permute-start(bf16[128,1024]{1,0:T(8,128)(2,1)S(1)} %get-tuple-element.28), channel_id=1, source_target_pairs={{0,4},{4,8},{8,12},{12,0},{1,5},{5,9},{9,13},{13,1},{2,6},{6,10},{... | collective-permute-start | bytes 786440 | tf_op jit(solution)/shard_map/ppermute | solution.py:28
  202.4 19.7 %collective-permute-start.14 = (bf16[128,1024]{1,0:T(8,128)(2,1)S(1)}, bf16[128,1024]{1,0:T(8,128)(2,1)S(1)}, u32[]{:S(2)}, u32[]{:S(2)}) collective-permute-start(bf16[128,1024]{1,0:T(8,128)(2,1)S(1)} %get-tuple-element.29), channel_id=1, source_target_pairs={{0,8},{4,12},{8,0},{12,4},{1,9},{5,13},{9,1},{13,5},{2,10},{6,14},... | collective-permute-start | bytes 786440 | tf_op jit(solution)/shard_map/ppermute | solution.py:28
  (25 other events, 198.7 us)
